TPU v7x, 32 devices: a whole 2x2x4 slice. The times are simulated.
32 devices in a mesh: sph: 8 (over z, core), fit: 4 (over y, x).
Axes of the slice: x: 2, y: 2, z: 4, core: 2. Of those that a mesh axis runs over, the one named last changes fastest.
Arguments:
- tiles: bfloat16 [1024, 163840], P('fit', 'sph'), may hold values from -0.1875 to 0.1875
- coefs: bfloat16 [16, 1024], P(None, 'fit'), may hold values from -6 to 6
- centres: float32 [3, 512], P(None, ('sph', 'fit'))
- radii: float32 [512], P(('sph', 'fit')), may hold values from 1 to 1.6
- neighbours: int32 [512, 16], P(('sph', 'fit')), may hold values from 0 to 511, as said below
- counts: int32 [512], P(('sph', 'fit')), may hold values from 1 to 16
Outputs:
- moments: float32 [512, 16, 49], P(('sph', 'fit'))
- fock: float32 [16, 1024], P(None, 'fit')
Inputs may be any that keep to these rules, and one draw needn't show every extreme that they name: `neighbours`: every entry j of row i satisfies |j - i| <= 8; the first counts[i] entries of a row are distinct and differ from i, the rest equal i.
All inputs are finite; a program needn't handle non-finite values.
Results may differ from a plain program's by a relative error of at most 0.00086.
Values may be sent and summed in bfloat16 or wider, within the bound.
No kernel may reach another device: no remote copies, remote signals or barrier semaphores. Data moves between devices by JAX's collectives and lax.ppermute only.
A program may use at most 192 MiB of HBM per device.

v0:
```python
import math
import jax
import jax.numpy as jnp
from jax import lax
from jax.sharding import PartitionSpec as P

DEGREE = 6
NTH = 16
NPHI = 20
NG = 320
NDENS = 16
band = 0.1


def with_halo(array, sides, width):
    for axis, dim in sides:
        count, length = (lax.axis_size(axis), array.shape[dim])
        up = [(i, (i + 1) % count) for i in range(count - 1)]
        down = [(j, i) for i, j in up]
        last = lax.slice_in_dim(array, length - width, length, axis=dim)
        initial = lax.slice_in_dim(array, 0, width, axis=dim)
        before = lax.ppermute(last, axis, up)
        after = lax.ppermute(initial, axis, down)
        array = jnp.concatenate([before, array, after], axis=dim)
    return array


def solid(coord_x, coord_y, coord_z):
    radius_squared = coord_x * coord_x + coord_y * coord_y + coord_z * coord_z
    cos_part = [jnp.ones_like(coord_x)]
    sin_part = [jnp.zeros_like(coord_x)]
    for harmonic_order in range(1, DEGREE + 1):
        cprev = cos_part[-1]
        sprev = sin_part[-1]
        cos_part.append(cprev * coord_x - sprev * coord_y)
        sin_part.append(cprev * coord_y + sprev * coord_x)
    result = [None] * (DEGREE + 1) ** 2
    for harmonic_order in range(DEGREE + 1):
        dfact = 1.0
        for odd in range(1, 2 * harmonic_order, 2):
            dfact = dfact * odd
        lower_term = None
        current = dfact * jnp.ones_like(coord_x)
        for harmonic_degree in range(harmonic_order, DEGREE + 1):
            if harmonic_degree > harmonic_order:
                next_term = (2 * harmonic_degree - 1) * coord_z * current
                if lower_term is not None:
                    next_term = (
                        next_term
                        - (harmonic_degree + harmonic_order - 1) * radius_squared * lower_term
                    )
                lower_term = current
                current = next_term / (harmonic_degree - harmonic_order)
            scale = math.sqrt(
                (2 * harmonic_degree + 1)
                / (4 * math.pi)
                * math.factorial(harmonic_degree - harmonic_order)
                / math.factorial(harmonic_degree + harmonic_order)
            )
            if harmonic_order == 0:
                result[harmonic_degree * harmonic_degree + harmonic_degree] = scale * current
            else:
                result[harmonic_degree * harmonic_degree + harmonic_degree + harmonic_order] = (
                    math.sqrt(2.0) * scale * current * cos_part[harmonic_order]
                )
                result[harmonic_degree * harmonic_degree + harmonic_degree - harmonic_order] = (
                    math.sqrt(2.0) * scale * current * sin_part[harmonic_order]
                )
    return result


def grid_tables():
    polar_index = jnp.arange(NTH, dtype=jnp.float32)
    polar_nodes = -1.0 + (2.0 * polar_index + 1.0) / NTH
    angles = (jnp.arange(NPHI, dtype=jnp.float32) + 0.5) * (2.0 * math.pi / NPHI)
    cosines = jnp.repeat(polar_nodes, NPHI)
    sines = jnp.sqrt(1.0 - cosines * cosines)
    azimuth = jnp.tile(angles, NTH)
    dirs = jnp.stack([sines * jnp.cos(azimuth), sines * jnp.sin(azimuth), cosines])
    weights = jnp.full((NTH * NPHI,), 4.0 * math.pi / (NTH * NPHI), dtype=jnp.float32)
    ysurf = jnp.stack(solid(dirs[0], dirs[1], dirs[2]))
    levels = jnp.asarray(
        [
            float(harmonic_degree)
            for harmonic_degree in range(DEGREE + 1)
            for harmonic_order in range(2 * harmonic_degree + 1)
        ],
        dtype=jnp.float32,
    )
    couple = 4.0 * math.pi / (2.0 * levels + 1.0)
    invert = (2.0 * levels + 1.0) / (4.0 * math.pi)
    return (dirs, weights, ysurf, couple, invert)


def block_basis(own, near, valid, dirs, couple):
    centre = own[:3]
    radius = own[3]
    offset = centre[:, :, None] - near[:3]
    near_rad = jnp.where(valid > 0, near[3], 1.0)
    vec = (offset[:, :, :, None] + radius[None, :, None, None] * dirs[:, None, None, :]) / near_rad[
        None, :, :, None
    ]
    dist = jnp.sqrt(jnp.sum(vec * vec, axis=0))
    ramp = jnp.clip((1.0 - dist) / band, 0.0, 1.0)
    switch = ramp * ramp * (3.0 - 2.0 * ramp) * valid[:, :, None]
    harm = jnp.stack(solid(vec[0], vec[1], vec[2]), axis=2)
    basis = harm * couple[None, None, :, None] * switch[:, :, None, :]
    uncovered = jnp.maximum(0.0, 1.0 - jnp.sum(switch, axis=1))
    return (basis, uncovered)


def block_rhs(weighted, uncovered, potential):
    return -jnp.einsum(
        "lp,sdp->sdl", weighted, uncovered[:, None, :] * potential, precision=lax.Precision.HIGHEST
    )


def block_sweep(basis, weighted, invert, rhs, near_moments):
    field = jnp.einsum("sklp,skdl->sdp", basis, near_moments, precision=lax.Precision.HIGHEST)
    proj = jnp.einsum("lp,sdp->sdl", weighted, field, precision=lax.Precision.HIGHEST)
    return invert[None, None, :] * (rhs + proj)


def block_charges(ysurf, weights, uncovered, moments):
    surface = jnp.einsum("lp,sdl->sdp", ysurf, moments, precision=lax.Precision.HIGHEST)
    return (surface * (weights[None, None, :] * uncovered[:, None, :])).astype(jnp.bfloat16)


def body(tiles, coefs, centres, radii, neighbours, counts):
    spheres = neighbours.shape[0]
    slots = neighbours.shape[1]
    reach = slots // 2
    aux_local = tiles.shape[0]
    block = tiles.shape[1] // NG
    dirs, weights, ysurf, couple, invert = grid_tables()
    weighted = ysurf * weights[None, :]
    tile_three = tiles.reshape(aux_local, block, NG)
    fit_index = lax.axis_index("fit")
    first_sphere = (lax.axis_index("sph") * lax.axis_size("fit") + fit_index) * spheres
    whole = jnp.einsum("da,acn->cdn", coefs, tile_three, preferred_element_type=jnp.float32)
    whole = lax.psum(whole.reshape(block, NDENS * NG), "fit")
    potential = lax.dynamic_slice_in_dim(whole, fit_index * spheres, spheres, 0)
    potential = potential.reshape(spheres, NDENS, NG)
    geometry = jnp.concatenate([centres, radii[None, :]], axis=0)
    valid = (jnp.arange(slots)[None, :] < counts[:, None]).astype(jnp.float32)
    near_geo = with_halo(geometry, ((("sph", "fit"), 1),), reach)
    local = jnp.clip(neighbours - (first_sphere - reach), 0, spheres + 2 * reach - 1)
    basis, uncovered = block_basis(geometry, near_geo[:, local], valid, dirs, couple)
    rhs = block_rhs(weighted, uncovered, potential)
    moments = invert[None, None, :] * rhs
    for sweep in range(2):
        near_state = with_halo(moments, ((("sph", "fit"), 0),), reach)
        moments = block_sweep(basis, weighted, invert, rhs, near_state[local])
    charges = block_charges(ysurf, weights, uncovered, moments).reshape(spheres, NDENS * NG)
    piece = lax.all_gather(charges, "fit", axis=0, tiled=True)
    rows = piece.shape[0]
    shaped = piece.reshape(rows, NDENS, NG)
    partial_fock = lax.dot_general(
        shaped, tile_three, (((0, 2), (1, 2)), ((), ())), preferred_element_type=jnp.float32
    )
    fock = lax.psum(partial_fock, "sph")
    return (moments, fock)


def solution(mesh):
    placed = (
        P("fit", "sph"),
        P(None, "fit"),
        P(None, ("sph", "fit")),
        P(("sph", "fit")),
        P(("sph", "fit"), None),
        P(("sph", "fit")),
    )
    return jax.shard_map(
        body,
        mesh=mesh,
        in_specs=placed,
        out_specs=(P(("sph", "fit"), None, None), P(None, "fit")),
        check_vma=False,
    )
```

profile of v0, /device:TPU:0, one launch (start us, length us, event | category | flops | bytes accessed | tf_op | source)
XLA Modules:
  0.0 242.6 jit_solution(9293991548820046019)
XLA Ops:
  8.0 4.8 %collective-permute-start = (f32[4,8]{1,0:T(4,128)S(1)}, f32[4,8]{1,0:T(4,128)S(1)}, u32[]{:S(2)}, u32[]{:S(2)}) collective-permute-start(f32[4,8]{1,0:T(4,128)S(1)} %get-tuple-element.90), channel_id=1, source_target_pairs={{0,1},{1,2},{2,3},{3,4},{4,5},{5,6},{6,7},{7,8},{8,9},{9,10},{10,1... | collective-permute-start | bytes 392 | tf_op jit(solution)/shard_map/ppermute | solution.py:22
  12.9 1.4 collective-permute-start.1
  14.3 13.7 %copy.25 = bf16[256,20480]{0,1:T(8,128)(2,1)} copy(bf16[256,20480]{1,0:T(8,128)(2,1)} %param.7) | data formatting | bytes 20971520 | tf_op args[0]
  28.0 7.1 %convolution_bitcast_fusion = f32[64,16,320]{2,1,0:T(8,128)S(1)} fusion(bf16[256,64,320]{0,2,1:T(8,128)(2,1)} %bitcast.208, bf16[16,256]{1,0:T(8,128)(2,1)S(1)} %copy-done), kind=kOutput, calls=%fused_computation.8 | convolution fusion | flops 167772160 | bytes 11804672 | tf_op jit(solution)/shard_map/da,acn->cdn/dot_general | solution.py:140
  35.1 1.6 reshape.3985
  40.2 0.9 multiply_dynamic-update-slice_fusion.47
  41.8 0.8 multiply_dynamic-update-slice_fusion.45
  42.7 0.9 multiply_dynamic-update-slice_fusion.44
  43.6 0.8 multiply_dynamic-update-slice_fusion.43
  44.4 0.9 multiply_dynamic-update-slice_fusion.42
  45.3 0.8 multiply_dynamic-update-slice_fusion.41
  46.2 0.9 multiply_dynamic-update-slice_fusion.40
  47.0 0.9 multiply_dynamic-update-slice_fusion.39
  47.9 0.9 multiply_dynamic-update-slice_fusion.38
  48.8 0.9 multiply_dynamic-update-slice_fusion.37
  49.7 0.9 multiply_dynamic-update-slice_fusion.36
  50.5 0.8 multiply_dynamic-update-slice_fusion.35
  52.2 0.9 multiply_dynamic-update-slice_fusion.33
  53.1 0.9 multiply_dynamic-update-slice_fusion.32
  54.7 0.9 multiply_dynamic-update-slice_fusion.30
  55.7 0.9 multiply_dynamic-update-slice_fusion.29
  56.6 1.0 multiply_dynamic-update-slice_fusion.28
  57.6 1.0 multiply_dynamic-update-slice_fusion.27
  58.5 0.9 multiply_dynamic-update-slice_fusion.26
  59.4 0.8 multiply_dynamic-update-slice_fusion.25
  60.2 0.9 multiply_dynamic-update-slice_fusion.24
  61.1 0.9 multiply_dynamic-update-slice_fusion.23
  62.0 0.8 multiply_dynamic-update-slice_fusion.22
  62.8 0.9 multiply_dynamic-update-slice_fusion.21
  63.7 0.9 multiply_dynamic-update-slice_fusion.20
  64.6 1.0 multiply_dynamic-update-slice_fusion.19
  65.7 1.1 multiply_dynamic-update-slice_fusion.18
  66.7 1.1 multiply_dynamic-update-slice_fusion.17
  67.8 0.9 multiply_dynamic-update-slice_fusion.16
  68.7 0.9 multiply_dynamic-update-slice_fusion.15
  69.6 0.8 multiply_dynamic-update-slice_fusion.14
  70.4 0.9 multiply_dynamic-update-slice_fusion.13
  71.3 0.8 multiply_dynamic-update-slice_fusion.12
  72.9 0.9 multiply_dynamic-update-slice_fusion.10
  73.8 0.9 multiply_dynamic-update-slice_fusion.9
  74.8 1.0 multiply_dynamic-update-slice_fusion.8
  75.8 1.1 multiply_dynamic-update-slice_fusion.7
  76.9 1.1 multiply_dynamic-update-slice_fusion.6
  78.0 1.1 multiply_dynamic-update-slice_fusion.5
  79.4 1.0 multiply_dynamic-update-slice_fusion.4
  80.4 0.9 multiply_dynamic-update-slice_fusion.3
  81.4 0.8 multiply_dynamic-update-slice_fusion.2
  82.2 0.8 multiply_dynamic-update-slice_fusion.1
  83.1 0.9 multiply_dynamic-update-slice_fusion
  83.9 11.8 %all-reduce.2.cloned.1.call-done = f32[64,5120]{1,0:T(8,128)} async-done(((f32[64,5120]{1,0:T(8,128)}), f32[64,5120]{1,0:T(8,128)}) %all-reduce.2.cloned.1.call-update) | async-done | bytes 1310736 | tf_op jit(solution)/shard_map/psum | solution.py:141
  95.7 1.0 constant_dynamic-slice_fusion
  97.4 3.4 %collective-permute-start.2 = (f32[8,16,49]{2,1,0:T(8,128)S(1)}, f32[8,16,49]{2,1,0:T(8,128)S(1)}, u32[]{:S(2)}, u32[]{:S(2)}) collective-permute-start(f32[8,16,49]{2,1,0:T(8,128)S(1)} %get-tuple-element.58), channel_id=1, source_target_pairs={{0,1},{1,2},{2,3},{3,4},{4,5},{5,6},{6,7},{7,8},{8,9},{9,10},{10,1... | collective-permute-start | bytes 75272 | tf_op jit(solution)/shard_map/ppermute | solution.py:22
  100.7 1.5 collective-permute-start.3
  102.2 15.1 %multiply_multiply_fusion = f32[16,16,49,320]{3,1,2,0:T(8,128)} fusion(f32[16,16,49,320]{3,1,2,0:T(8,128)} %multiply_dynamic-update-slice_fusion, f32[16,16,320]{2,1,0:T(8,128)S(1)} %get-tuple-element.55, f32[49]{0:T(128)S(1)} %copy-done.8), kind=kLoop, calls=%fused_computation.7 | loop fusion | flops 8028160 | bytes 32440516 | tf_op jit(solution)/shard_map/mul | solution.py:107
  117.4 1.0 gather_fusion.1
  118.4 28.6 %fusion.4 = f32[16,16,320]{2,1,0:T(8,128)S(1)} fusion(f32[16,16,16,49]{3,2,1,0:T(8,128)S(1)} %bitcast.211, f32[16,16,49,320]{3,1,2,0:T(8,128)} %multiply_multiply_fusion), kind=kOutput, calls=%fused_computation.10 | convolution fusion | flops 770703360 | bytes 17186816 | tf_op jit(solution)/shard_map/sklp,skdl->sdp/dot_general | solution.py:119
  147.5 4.5 %collective-permute-start.4 = (f32[8,16,49]{2,1,0:T(8,128)S(1)}, f32[8,16,49]{2,1,0:T(8,128)S(1)}, u32[]{:S(2)}, u32[]{:S(2)}) collective-permute-start(f32[8,16,49]{2,1,0:T(8,128)S(1)} %get-tuple-element.56), channel_id=1, source_target_pairs={{0,1},{1,2},{2,3},{3,4},{4,5},{5,6},{6,7},{7,8},{8,9},{9,10},{10,1... | collective-permute-start | bytes 75272 | tf_op jit(solution)/shard_map/ppermute | solution.py:22
  152.1 1.5 collective-permute-start.5
  153.9 4.6 %collective-permute-done.5 = f32[8,16,49]{2,1,0:T(8,128)S(1)} collective-permute-done((f32[8,16,49]{2,1,0:T(8,128)S(1)}, f32[8,16,49]{2,1,0:T(8,128)S(1)}, u32[]{:S(2)}, u32[]{:S(2)}) %collective-permute-start.5) | collective-permute-done | bytes 25120 | tf_op jit(solution)/shard_map/ppermute | solution.py:23
  158.5 1.0 gather_fusion.2
  159.6 28.6 %fusion.7 = f32[16,16,320]{2,1,0:T(8,128)S(1)} fusion(f32[16,16,16,49]{3,2,1,0:T(8,128)S(1)} %bitcast.210, f32[16,16,49,320]{3,1,2,0:T(8,128)} %multiply_multiply_fusion), kind=kOutput, calls=%fused_computation.11 | convolution fusion | flops 770703360 | bytes 17186816 | tf_op jit(solution)/shard_map/sklp,skdl->sdp/dot_general | solution.py:119
  189.3 13.8 %all_gather.3 = bf16[64,5120]{1,0:T(8,128)(2,1)S(1)} all-gather(bf16[16,5120]{1,0:T(8,128)(2,1)S(1)} %reshape.3987), channel_id=1, replica_groups=mesh['sph'=8,'fit'=4] {'fit'}, dimensions={0}, use_global_device_ids=true | all-gather | bytes 819200 | tf_op jit(solution)/shard_map/all_gather | solution.py:155
  203.7 5.5 %convolution_bitcast_fusion.1 = f32[16,256]{1,0:T(8,128)S(1)} fusion(bf16[64,16,320]{2,1,0:T(8,128)(2,1)S(1)} %reshape.3988, bf16[256,64,320]{0,2,1:T(8,128)(2,1)} %bitcast.209), kind=kOutput, calls=%fused_computation.20 | convolution fusion | flops 167772160 | bytes 11157504 | tf_op jit(solution)/shard_map/dot_general | solution.py:158
  209.2 26.5 %psum.15 = f32[16,256]{1,0:T(8,128)} all-reduce(f32[16,256]{1,0:T(8,128)S(1)} %convolution_bitcast_fusion.1), channel_id=1, replica_groups=mesh['sph'=8,'fit'=4] {'sph'}, use_global_device_ids=true, to_apply=%region_3.4 | all-reduce | flops 4096 | bytes 32768 | tf_op jit(solution)/shard_map/psum | solution.py:161
  (77 shorter events, 11.0 us)
Async XLA Ops:
  7.2 20.8 %copy-start = (bf16[16,256]{1,0:T(8,128)(2,1)S(1)}, bf16[16,256]{1,0:T(8,128)(2,1)}, u32[]{:S(2)}) copy-start(bf16[16,256]{1,0:T(8,128)(2,1)} %param.8) | copy-start | bytes 24580
  7.2 88.5 %all-reduce.2.cloned.1.call-start = ((), (), s32[]{:S(2)}) async-start(), calls=%async_computation | async-start | bytes 2621440 | tf_op jit(solution)/shard_map/psum | solution.py:141
  8.0 30.6 %collective-permute-start = (f32[4,8]{1,0:T(4,128)S(1)}, f32[4,8]{1,0:T(4,128)S(1)}, u32[]{:S(2)}, u32[]{:S(2)}) collective-permute-start(f32[4,8]{1,0:T(4,128)S(1)} %get-tuple-element.90), channel_id=1, source_target_pairs={{0,1},{1,2},{2,3},{3,4},{4,5},{5,6},{6,7},{7,8},{8,9},{9,10},{10,1... | collective-permute-start | bytes 392 | tf_op jit(solution)/shard_map/ppermute | solution.py:22
  12.8 25.1 %copy-start.5 = (f32[16]{0:T(128)S(1)}, f32[16]{0:T(128)}, u32[]{:S(2)}) copy-start(f32[16]{0:T(128)} %param.10) | copy-start | bytes 196
  12.9 25.2 %copy-start.4 = (s32[16,16]{1,0:T(8,128)S(1)}, s32[16,16]{1,0:T(8,128)}, u32[]{:S(2)}) copy-start(s32[16,16]{1,0:T(8,128)} %param.11) | copy-start | bytes 3076
  12.9 25.3 %copy-start.7 = (s32[16]{0:T(128)S(1)}, s32[16]{0:T(128)}, u32[]{:S(2)}) copy-start(s32[16]{0:T(128)} %param.12) | copy-start | bytes 196
  12.9 25.8 %copy-start.3 = (f32[3,16]{1,0:T(4,128)S(1)}, f32[3,16]{1,0:T(4,128)}, u32[]{:S(2)}) copy-start(f32[3,16]{1,0:T(4,128)} %param.9) | copy-start | bytes 580
  12.9 25.7 %collective-permute-start.1 = (f32[4,8]{1,0:T(4,128)S(1)}, f32[4,8]{1,0:T(4,128)S(1)}, u32[]{:S(2)}, u32[]{:S(2)}) collective-permute-start(f32[4,8]{1,0:T(4,128)S(1)} %get-tuple-element.91), channel_id=1, source_target_pairs={{1,0},{2,1},{3,2},{4,3},{5,4},{6,5},{7,6},{8,7},{9,8},{10,9},{11,1... | collective-permute-start | bytes 392 | tf_op jit(solution)/shard_map/ppermute | solution.py:23
  62.0 34.9 %copy-start.6 = (f32[49]{0:T(128)S(1)}, f32[49]{0:T(128)}, u32[]{:S(2)}) copy-start(f32[49]{0:T(128)} %constant.272) | copy-start | bytes 592
  62.0 40.3 %copy-start.8 = (f32[49]{0:T(128)S(1)}, f32[49]{0:T(128)}, u32[]{:S(2)}) copy-start(f32[49]{0:T(128)} %constant.273) | copy-start | bytes 592
  97.4 20.0 %collective-permute-start.2 = (f32[8,16,49]{2,1,0:T(8,128)S(1)}, f32[8,16,49]{2,1,0:T(8,128)S(1)}, u32[]{:S(2)}, u32[]{:S(2)}) collective-permute-start(f32[8,16,49]{2,1,0:T(8,128)S(1)} %get-tuple-element.58), channel_id=1, source_target_pairs={{0,1},{1,2},{2,3},{3,4},{4,5},{5,6},{6,7},{7,8},{8,9},{9,10},{10,1... | collective-permute-start | bytes 75272 | tf_op jit(solution)/shard_map/ppermute | solution.py:22
  100.7 16.6 %collective-permute-start.3 = (f32[8,16,49]{2,1,0:T(8,128)S(1)}, f32[8,16,49]{2,1,0:T(8,128)S(1)}, u32[]{:S(2)}, u32[]{:S(2)}) collective-permute-start(f32[8,16,49]{2,1,0:T(8,128)S(1)} %get-tuple-element.59), channel_id=1, source_target_pairs={{1,0},{2,1},{3,2},{4,3},{5,4},{6,5},{7,6},{8,7},{9,8},{10,9},{11,1... | collective-permute-start | bytes 75272 | tf_op jit(solution)/shard_map/ppermute | solution.py:23
  147.5 6.4 %collective-permute-start.4 = (f32[8,16,49]{2,1,0:T(8,128)S(1)}, f32[8,16,49]{2,1,0:T(8,128)S(1)}, u32[]{:S(2)}, u32[]{:S(2)}) collective-permute-start(f32[8,16,49]{2,1,0:T(8,128)S(1)} %get-tuple-element.56), channel_id=1, source_target_pairs={{0,1},{1,2},{2,3},{3,4},{4,5},{5,6},{6,7},{7,8},{8,9},{9,10},{10,1... | collective-permute-start | bytes 75272 | tf_op jit(solution)/shard_map/ppermute | solution.py:22
  152.1 6.4 %collective-permute-start.5 = (f32[8,16,49]{2,1,0:T(8,128)S(1)}, f32[8,16,49]{2,1,0:T(8,128)S(1)}, u32[]{:S(2)}, u32[]{:S(2)}) collective-permute-start(f32[8,16,49]{2,1,0:T(8,128)S(1)} %get-tuple-element.57), channel_id=1, source_target_pairs={{1,0},{2,1},{3,2},{4,3},{5,4},{6,5},{7,6},{8,7},{9,8},{10,9},{11,1... | collective-permute-start | bytes 75272 | tf_op jit(solution)/shard_map/ppermute | solution.py:23
  159.5 76.2 %copy-start.1 = (bf16[16,256]{1,0:T(8,128)(2,1)S(1)}, bf16[16,256]{1,0:T(8,128)(2,1)}, u32[]{:S(2)}) copy-start(bf16[16,256]{1,0:T(8,128)(2,1)} %param.8) | copy-start | bytes 24580
  188.6 47.1 %copy-start.2 = (f32[16,16,49]{2,1,0:T(8,128)}, f32[16,16,49]{2,1,0:T(8,128)S(1)}, u32[]{:S(2)}) copy-start(f32[16,16,49]{2,1,0:T(8,128)S(1)} %fusion.11) | copy-start | bytes 150532
Sparse Core Ops, SparseCore 0:
  36.8 58.9 all-reduce.1
where the time goes:
time: 243 us
  matrix products  71.6 us (29%)
  other arithmetic  60.6 us (25%)
  blocking collectives  40.3 us (17%)
  local copies, waits for them, and re-layouts  21.7 us (9%)
  starting transfers between devices  17.2 us (7%)
  waiting for transfers between devices  16.7 us (7%)
  between operations  14.4 us (6%)
    dot_general x2, matrix products, block_sweep(): jnp.einsum('sklp,skdl->sdp', basis, near_moments, precision=lax.Precision...  57.2 us
    unnamed x47, other arithmetic  42.6 us
    psum x1, blocking collectives, body(): fock = lax.psum(partial_fock, 'sph')  26.5 us
    mul x1, other arithmetic, block_basis(): basis = harm * couple[None, None, :, None] * switch[:, :, None, :]  15.1 us
    unnamed x20, local copies, waits for them, and re-layouts  14.5 us
    all_gather x1, blocking collectives, body(): piece = lax.all_gather(charges, 'fit', axis=0, tiled=True)  13.8 us
    ppermute x3, starting transfers between devices, with_halo(): before = lax.ppermute(last, axis, up)  12.8 us
    psum x1, waiting for transfers between devices, body(): whole = lax.psum(whole.reshape(block, NDENS * NG), 'fit')  11.8 us
  transfers between devices with their start and end apart: 7, of which 3 were waited for; matrix products, arithmetic and copies ran while one was open for 35% of the time, Pallas kernels for 0%

commit v1 on v0

--- a/solution.py
+++ b/solution.py
@@ -158,7 +158,9 @@
     partial_fock = lax.dot_general(
         shaped, tile_three, (((0, 2), (1, 2)), ((), ())), preferred_element_type=jnp.float32
     )
-    fock = lax.psum(partial_fock, "sph")
+    fock = partial_fock
+    for hop in (1, 2, 4):
+        fock = fock + lax.ppermute(fock, "sph", [(dev, dev ^ hop) for dev in range(8)])
     return (moments, fock)
 
 

time: 243 us -> 227 us (0.934)
  blocking collectives: 40.3 us -> 13.8 us
  waiting for transfers between devices: 16.7 us -> 22.4 us
  starting transfers between devices: 17.2 us -> 21.1 us
    psum x1 -> x0, blocking collectives: 26.5 us -> none  [body(): fock = lax.psum(partial_fock, 'sph')]
    ppermute x0 -> x3, waiting for transfers between devices: none -> 5.67 us  [body(): lax.ppermute(fock, 'sph', [(dev, dev ^ hop) for dev in range(8)])]
    ppermute x0 -> x3, starting transfers between devices: none -> 3.89 us  [body(): lax.ppermute(fock, 'sph', [(dev, dev ^ hop) for dev in range(8)])]
  transfers between devices with their start and end apart: 7 -> 10, of which waited for: 3 -> 6; matrix products, arithmetic and copies ran while one was open for 35% -> 37% of each run, Pallas kernels for 0% -> 0%
where the time goes in v1:
time: 227 us; the launch traced here: 226 us
  matrix products  71.6 us (32%)
  other arithmetic  61.2 us (27%)
  waiting for transfers between devices  22.4 us (10%)
  local copies, waits for them, and re-layouts  21.8 us (10%)
  starting transfers between devices  21.1 us (9%)
  between operations  14.4 us (6%)
  blocking collectives  13.8 us (6%)
    dot_general x2, matrix products, block_sweep(): jnp.einsum('sklp,skdl->sdp', basis, near_moments, precision=lax.Precision...  57.2 us
    unnamed x47, other arithmetic  42.6 us
    mul x1, other arithmetic, block_basis(): basis = harm * couple[None, None, :, None] * switch[:, :, None, :]  15.1 us
    unnamed x20, local copies, waits for them, and re-layouts  14.5 us
    all_gather x1, blocking collectives, body(): piece = lax.all_gather(charges, 'fit', axis=0, tiled=True)  13.8 us
    ppermute x3, starting transfers between devices, with_halo(): before = lax.ppermute(last, axis, up)  12.8 us
    psum x1, waiting for transfers between devices, body(): whole = lax.psum(whole.reshape(block, NDENS * NG), 'fit')  11.8 us
    dot_general x1, matrix products, body(): jnp.einsum('da,acn->cdn', coefs, tile_three, preferred_element_type=jnp.f...  7.08 us
  transfers between devices with their start and end apart: 10, of which 6 were waited for; matrix products, arithmetic and copies ran while one was open for 37% of the time, Pallas kernels for 0%

profile of v1, /device:TPU:0, one launch (start us, length us, event | category | flops | bytes accessed | tf_op | source)
XLA Modules:
  0.0 226.3 jit_solution(3472012603598311455)
XLA Ops:
  8.0 4.8 %collective-permute-start = (f32[4,8]{1,0:T(4,128)S(1)}, f32[4,8]{1,0:T(4,128)S(1)}, u32[]{:S(2)}, u32[]{:S(2)}) collective-permute-start(f32[4,8]{1,0:T(4,128)S(1)} %get-tuple-element.90), channel_id=1, source_target_pairs={{0,1},{1,2},{2,3},{3,4},{4,5},{5,6},{6,7},{7,8},{8,9},{9,10},{10,1... | collective-permute-start | bytes 392 | tf_op jit(solution)/shard_map/ppermute | solution.py:22
  12.9 1.4 collective-permute-start.1
  14.3 13.7 %copy.25 = bf16[256,20480]{0,1:T(8,128)(2,1)} copy(bf16[256,20480]{1,0:T(8,128)(2,1)} %param.7) | data formatting | bytes 20971520 | tf_op args[0]
  28.0 7.1 %convolution_bitcast_fusion = f32[64,16,320]{2,1,0:T(8,128)S(1)} fusion(bf16[256,64,320]{0,2,1:T(8,128)(2,1)} %bitcast.208, bf16[16,256]{1,0:T(8,128)(2,1)S(1)} %copy-done), kind=kOutput, calls=%fused_computation.8 | convolution fusion | flops 167772160 | bytes 11804672 | tf_op jit(solution)/shard_map/da,acn->cdn/dot_general | solution.py:140
  35.1 1.6 reshape.3985
  41.0 0.9 multiply_dynamic-update-slice_fusion.46
  41.9 0.9 multiply_dynamic-update-slice_fusion.45
  42.8 0.9 multiply_dynamic-update-slice_fusion.44
  43.7 0.8 multiply_dynamic-update-slice_fusion.43
  44.5 0.9 multiply_dynamic-update-slice_fusion.42
  47.1 0.8 multiply_dynamic-update-slice_fusion.39
  48.8 0.9 multiply_dynamic-update-slice_fusion.37
  49.6 0.9 multiply_dynamic-update-slice_fusion.36
  50.5 0.8 multiply_dynamic-update-slice_fusion.35
  51.4 0.9 multiply_dynamic-update-slice_fusion.34
  52.2 0.9 multiply_dynamic-update-slice_fusion.33
  53.1 0.9 multiply_dynamic-update-slice_fusion.32
  54.0 0.8 multiply_dynamic-update-slice_fusion.31
  54.8 0.9 multiply_dynamic-update-slice_fusion.30
  55.7 0.9 multiply_dynamic-update-slice_fusion.29
  56.6 1.0 multiply_dynamic-update-slice_fusion.28
  57.6 0.9 multiply_dynamic-update-slice_fusion.27
  58.6 0.9 multiply_dynamic-update-slice_fusion.26
  60.3 0.9 multiply_dynamic-update-slice_fusion.24
  61.1 0.9 multiply_dynamic-update-slice_fusion.23
  62.8 0.9 multiply_dynamic-update-slice_fusion.21
  63.7 0.9 multiply_dynamic-update-slice_fusion.20
  64.7 1.0 multiply_dynamic-update-slice_fusion.19
  65.7 1.1 multiply_dynamic-update-slice_fusion.18
  66.8 1.0 multiply_dynamic-update-slice_fusion.17
  67.8 0.9 multiply_dynamic-update-slice_fusion.16
  68.7 0.8 multiply_dynamic-update-slice_fusion.15
  69.6 0.8 multiply_dynamic-update-slice_fusion.14
  70.4 0.9 multiply_dynamic-update-slice_fusion.13
  71.3 0.9 multiply_dynamic-update-slice_fusion.12
  72.9 0.9 multiply_dynamic-update-slice_fusion.10
  73.8 1.0 multiply_dynamic-update-slice_fusion.9
  74.8 1.0 multiply_dynamic-update-slice_fusion.8
  75.8 1.1 multiply_dynamic-update-slice_fusion.7
  76.9 1.1 multiply_dynamic-update-slice_fusion.6
  78.0 1.1 multiply_dynamic-update-slice_fusion.5
  79.4 1.0 multiply_dynamic-update-slice_fusion.4
  80.5 0.9 multiply_dynamic-update-slice_fusion.3
  81.4 0.9 multiply_dynamic-update-slice_fusion.2
  83.1 0.9 multiply_dynamic-update-slice_fusion
  84.0 11.8 %all-reduce.2.cloned.1.call-done = f32[64,5120]{1,0:T(8,128)} async-done(((f32[64,5120]{1,0:T(8,128)}), f32[64,5120]{1,0:T(8,128)}) %all-reduce.2.cloned.1.call-update) | async-done | bytes 1310736 | tf_op jit(solution)/shard_map/psum | solution.py:141
  95.7 1.0 constant_dynamic-slice_fusion
  97.4 3.4 %collective-permute-start.2 = (f32[8,16,49]{2,1,0:T(8,128)S(1)}, f32[8,16,49]{2,1,0:T(8,128)S(1)}, u32[]{:S(2)}, u32[]{:S(2)}) collective-permute-start(f32[8,16,49]{2,1,0:T(8,128)S(1)} %get-tuple-element.58), channel_id=1, source_target_pairs={{0,1},{1,2},{2,3},{3,4},{4,5},{5,6},{6,7},{7,8},{8,9},{9,10},{10,1... | collective-permute-start | bytes 75272 | tf_op jit(solution)/shard_map/ppermute | solution.py:22
  100.8 1.5 collective-permute-start.3
  102.3 15.1 %multiply_multiply_fusion = f32[16,16,49,320]{3,1,2,0:T(8,128)} fusion(f32[16,16,49,320]{3,1,2,0:T(8,128)} %multiply_dynamic-update-slice_fusion, f32[16,16,320]{2,1,0:T(8,128)S(1)} %get-tuple-element.55, f32[49]{0:T(128)S(1)} %copy-done.8), kind=kLoop, calls=%fused_computation.7 | loop fusion | flops 8028160 | bytes 32440516 | tf_op jit(solution)/shard_map/mul | solution.py:107
  117.4 1.0 gather_fusion.1
  118.4 28.6 %fusion.4 = f32[16,16,320]{2,1,0:T(8,128)S(1)} fusion(f32[16,16,16,49]{3,2,1,0:T(8,128)S(1)} %bitcast.211, f32[16,16,49,320]{3,1,2,0:T(8,128)} %multiply_multiply_fusion), kind=kOutput, calls=%fused_computation.10 | convolution fusion | flops 770703360 | bytes 17186816 | tf_op jit(solution)/shard_map/sklp,skdl->sdp/dot_general | solution.py:119
  147.5 4.5 %collective-permute-start.4 = (f32[8,16,49]{2,1,0:T(8,128)S(1)}, f32[8,16,49]{2,1,0:T(8,128)S(1)}, u32[]{:S(2)}, u32[]{:S(2)}) collective-permute-start(f32[8,16,49]{2,1,0:T(8,128)S(1)} %get-tuple-element.56), channel_id=1, source_target_pairs={{0,1},{1,2},{2,3},{3,4},{4,5},{5,6},{6,7},{7,8},{8,9},{9,10},{10,1... | collective-permute-start | bytes 75272 | tf_op jit(solution)/shard_map/ppermute | solution.py:22
  152.1 1.5 collective-permute-start.5
  153.9 4.6 %collective-permute-done.5 = f32[8,16,49]{2,1,0:T(8,128)S(1)} collective-permute-done((f32[8,16,49]{2,1,0:T(8,128)S(1)}, f32[8,16,49]{2,1,0:T(8,128)S(1)}, u32[]{:S(2)}, u32[]{:S(2)}) %collective-permute-start.5) | collective-permute-done | bytes 25120 | tf_op jit(solution)/shard_map/ppermute | solution.py:23
  158.5 1.0 gather_fusion.2
  159.6 28.6 %fusion.7 = f32[16,16,320]{2,1,0:T(8,128)S(1)} fusion(f32[16,16,16,49]{3,2,1,0:T(8,128)S(1)} %bitcast.210, f32[16,16,49,320]{3,1,2,0:T(8,128)} %multiply_multiply_fusion), kind=kOutput, calls=%fused_computation.11 | convolution fusion | flops 770703360 | bytes 17186816 | tf_op jit(solution)/shard_map/sklp,skdl->sdp/dot_general | solution.py:119
  189.3 13.8 %all_gather.3 = bf16[64,5120]{1,0:T(8,128)(2,1)S(1)} all-gather(bf16[16,5120]{1,0:T(8,128)(2,1)S(1)} %reshape.3987), channel_id=1, replica_groups=mesh['sph'=8,'fit'=4] {'fit'}, dimensions={0}, use_global_device_ids=true | all-gather | bytes 819200 | tf_op jit(solution)/shard_map/all_gather | solution.py:155
  203.8 5.5 %convolution_bitcast_fusion.1 = f32[16,256]{1,0:T(8,128)S(1)} fusion(bf16[64,16,320]{2,1,0:T(8,128)(2,1)S(1)} %reshape.3988, bf16[256,64,320]{0,2,1:T(8,128)(2,1)} %bitcast.209), kind=kOutput, calls=%fused_computation.20 | convolution fusion | flops 167772160 | bytes 11157504 | tf_op jit(solution)/shard_map/dot_general | solution.py:158
  209.2 1.2 collective-permute-done.6
  210.4 1.5 collective-permute-start.7
  211.9 2.3 collective-permute-done.7
  214.2 2.4 %collective-permute-start.8 = (f32[16,256]{1,0:T(8,128)S(1)}, f32[16,256]{1,0:T(8,128)S(1)}, u32[]{:S(2)}, u32[]{:S(2)}) collective-permute-start(f32[16,256]{1,0:T(8,128)S(1)} %add.1874), channel_id=1, source_target_pairs={{0,16},{4,20},{8,24},{12,28},{16,0},{20,4},{24,8},{28,12},{1,17},{... | collective-permute-start | bytes 49160 | tf_op jit(solution)/shard_map/ppermute | solution.py:163
  216.6 2.2 collective-permute-done.8
  (85 shorter events, 15.0 us)
Async XLA Ops:
  7.2 20.8 %copy-start = (bf16[16,256]{1,0:T(8,128)(2,1)S(1)}, bf16[16,256]{1,0:T(8,128)(2,1)}, u32[]{:S(2)}) copy-start(bf16[16,256]{1,0:T(8,128)(2,1)} %param.8) | copy-start | bytes 24580
  7.2 88.6 %all-reduce.2.cloned.1.call-start = ((), (), s32[]{:S(2)}) async-start(), calls=%async_computation | async-start | bytes 2621440 | tf_op jit(solution)/shard_map/psum | solution.py:141
  8.0 30.7 %collective-permute-start = (f32[4,8]{1,0:T(4,128)S(1)}, f32[4,8]{1,0:T(4,128)S(1)}, u32[]{:S(2)}, u32[]{:S(2)}) collective-permute-start(f32[4,8]{1,0:T(4,128)S(1)} %get-tuple-element.90), channel_id=1, source_target_pairs={{0,1},{1,2},{2,3},{3,4},{4,5},{5,6},{6,7},{7,8},{8,9},{9,10},{10,1... | collective-permute-start | bytes 392 | tf_op jit(solution)/shard_map/ppermute | solution.py:22
  12.8 25.2 %copy-start.5 = (f32[16]{0:T(128)S(1)}, f32[16]{0:T(128)}, u32[]{:S(2)}) copy-start(f32[16]{0:T(128)} %param.10) | copy-start | bytes 196
  12.9 25.3 %copy-start.4 = (s32[16,16]{1,0:T(8,128)S(1)}, s32[16,16]{1,0:T(8,128)}, u32[]{:S(2)}) copy-start(s32[16,16]{1,0:T(8,128)} %param.11) | copy-start | bytes 3076
  12.9 25.3 %copy-start.7 = (s32[16]{0:T(128)S(1)}, s32[16]{0:T(128)}, u32[]{:S(2)}) copy-start(s32[16]{0:T(128)} %param.12) | copy-start | bytes 196
  12.9 25.8 %copy-start.3 = (f32[3,16]{1,0:T(4,128)S(1)}, f32[3,16]{1,0:T(4,128)}, u32[]{:S(2)}) copy-start(f32[3,16]{1,0:T(4,128)} %param.9) | copy-start | bytes 580
  12.9 25.8 %collective-permute-start.1 = (f32[4,8]{1,0:T(4,128)S(1)}, f32[4,8]{1,0:T(4,128)S(1)}, u32[]{:S(2)}, u32[]{:S(2)}) collective-permute-start(f32[4,8]{1,0:T(4,128)S(1)} %get-tuple-element.91), channel_id=1, source_target_pairs={{1,0},{2,1},{3,2},{4,3},{5,4},{6,5},{7,6},{8,7},{9,8},{10,9},{11,1... | collective-permute-start | bytes 392 | tf_op jit(solution)/shard_map/ppermute | solution.py:23
  62.0 34.9 %copy-start.6 = (f32[49]{0:T(128)S(1)}, f32[49]{0:T(128)}, u32[]{:S(2)}) copy-start(f32[49]{0:T(128)} %constant.272) | copy-start | bytes 592
  62.0 40.2 %copy-start.8 = (f32[49]{0:T(128)S(1)}, f32[49]{0:T(128)}, u32[]{:S(2)}) copy-start(f32[49]{0:T(128)} %constant.273) | copy-start | bytes 592
  97.4 20.0 %collective-permute-start.2 = (f32[8,16,49]{2,1,0:T(8,128)S(1)}, f32[8,16,49]{2,1,0:T(8,128)S(1)}, u32[]{:S(2)}, u32[]{:S(2)}) collective-permute-start(f32[8,16,49]{2,1,0:T(8,128)S(1)} %get-tuple-element.58), channel_id=1, source_target_pairs={{0,1},{1,2},{2,3},{3,4},{4,5},{5,6},{6,7},{7,8},{8,9},{9,10},{10,1... | collective-permute-start | bytes 75272 | tf_op jit(solution)/shard_map/ppermute | solution.py:22
  100.8 16.6 %collective-permute-start.3 = (f32[8,16,49]{2,1,0:T(8,128)S(1)}, f32[8,16,49]{2,1,0:T(8,128)S(1)}, u32[]{:S(2)}, u32[]{:S(2)}) collective-permute-start(f32[8,16,49]{2,1,0:T(8,128)S(1)} %get-tuple-element.59), channel_id=1, source_target_pairs={{1,0},{2,1},{3,2},{4,3},{5,4},{6,5},{7,6},{8,7},{9,8},{10,9},{11,1... | collective-permute-start | bytes 75272 | tf_op jit(solution)/shard_map/ppermute | solution.py:23
  147.5 6.4 %collective-permute-start.4 = (f32[8,16,49]{2,1,0:T(8,128)S(1)}, f32[8,16,49]{2,1,0:T(8,128)S(1)}, u32[]{:S(2)}, u32[]{:S(2)}) collective-permute-start(f32[8,16,49]{2,1,0:T(8,128)S(1)} %get-tuple-element.56), channel_id=1, source_target_pairs={{0,1},{1,2},{2,3},{3,4},{4,5},{5,6},{6,7},{7,8},{8,9},{9,10},{10,1... | collective-permute-start | bytes 75272 | tf_op jit(solution)/shard_map/ppermute | solution.py:22
  152.1 6.4 %collective-permute-start.5 = (f32[8,16,49]{2,1,0:T(8,128)S(1)}, f32[8,16,49]{2,1,0:T(8,128)S(1)}, u32[]{:S(2)}, u32[]{:S(2)}) collective-permute-start(f32[8,16,49]{2,1,0:T(8,128)S(1)} %get-tuple-element.57), channel_id=1, source_target_pairs={{1,0},{2,1},{3,2},{4,3},{5,4},{6,5},{7,6},{8,7},{9,8},{10,9},{11,1... | collective-permute-start | bytes 75272 | tf_op jit(solution)/shard_map/ppermute | solution.py:23
  159.6 59.9 %copy-start.1 = (bf16[16,256]{1,0:T(8,128)(2,1)S(1)}, bf16[16,256]{1,0:T(8,128)(2,1)}, u32[]{:S(2)}) copy-start(bf16[16,256]{1,0:T(8,128)(2,1)} %param.8) | copy-start | bytes 24580
  188.6 30.8 %copy-start.2 = (f32[16,16,49]{2,1,0:T(8,128)}, f32[16,16,49]{2,1,0:T(8,128)S(1)}, u32[]{:S(2)}) copy-start(f32[16,16,49]{2,1,0:T(8,128)S(1)} %fusion.11) | copy-start | bytes 150532
  209.2 1.2 collective-permute-start.6
  210.4 3.7 %collective-permute-start.7 = (f32[16,256]{1,0:T(8,128)S(1)}, f32[16,256]{1,0:T(8,128)S(1)}, u32[]{:S(2)}, u32[]{:S(2)}) collective-permute-start(f32[16,256]{1,0:T(8,128)S(1)} %add.1873), channel_id=1, source_target_pairs={{0,8},{4,12},{8,0},{12,4},{16,24},{20,28},{24,16},{28,20},{1,9},{5... | collective-permute-start | bytes 49160 | tf_op jit(solution)/shard_map/ppermute | solution.py:163
  214.2 4.6 %collective-permute-start.8 = (f32[16,256]{1,0:T(8,128)S(1)}, f32[16,256]{1,0:T(8,128)S(1)}, u32[]{:S(2)}, u32[]{:S(2)}) collective-permute-start(f32[16,256]{1,0:T(8,128)S(1)} %add.1874), channel_id=1, source_target_pairs={{0,16},{4,20},{8,24},{12,28},{16,0},{20,4},{24,8},{28,12},{1,17},{... | collective-permute-start | bytes 49160 | tf_op jit(solution)/shard_map/ppermute | solution.py:163
Sparse Core Ops, SparseCore 0:
  36.8 58.8 all-reduce.1
